TPU v7x, 32 devices: a whole 2x2x4 slice. The times are simulated.
32 devices in a mesh: seq: 16 (over z, y, x), head: 2 (over core).
Axes of the slice: x: 2, y: 2, z: 4, core: 2. Of those that a mesh axis runs over, the one named last changes fastest.
Arguments:
- queries: bfloat16 [6144, 2048], P('seq', 'head'), may hold values from -6 to 6
- keys: bfloat16 [6144, 2048], P('seq', 'head'), may hold values from -0.5 to 0.5
- values: bfloat16 [6144, 2048], P('seq', 'head'), may hold values from -6 to 6
- level_pattern: int32 [6144], P('seq'), may hold values from 0 to 15
- level_weight: float32 [16, 9], replicated, may hold values from 0.5 to 2
- out_weight: bfloat16 [2, 1024, 2048], P('head', 'seq'), may hold values from -0.125 to 0.125
Outputs:
- mixed: float32 [6144, 2048], P('seq', 'head')
All inputs are finite; a program needn't handle non-finite values.
Results may differ from a plain program's by a relative error of at most 0.003.
Values may be sent and summed in bfloat16 or wider, within the bound.
A program may use at most 64 MiB of HBM per device.

v0:
```python
import functools
import itertools
import math

import jax
import jax.numpy as jnp
from jax import lax
from jax.experimental import pallas as pl
from jax.experimental.pallas import tpu as pltpu
from jax.sharding import PartitionSpec as P

HD = 128
MESH = pl.DeviceIdType.MESH


def line_dims(mesh):
    n = mesh.shape["seq"]
    devices = mesh.devices.reshape(n, -1)[:, 0]
    coords = [tuple(getattr(d, "coords", ())) for d in devices]
    dims = []
    if len(set(coords)) == n:
        for axis in range(len(coords[0])):
            seen = [c[axis] - coords[0][axis] for c in coords]
            length = max(seen) + 1
            if length > 1:
                dims.append((length, seen.index(1)))
    stride = 1
    for length, step in sorted(dims, key=lambda d: d[1]):
        if step != stride:
            break
        stride *= length
    if not dims or stride != n:
        dims = [(2, 1 << i) for i in range(n.bit_length() - 1)]
    return sorted(dims, key=lambda d: -d[1])


def nearest(k, p, n):
    m = jnp.minimum(p, n - 1 - p)
    sign = jnp.where(p == m, 1, -1)
    near = (k + 1) // 2 * (2 * (k % 2) - 1)
    if n == 2:
        return p + k * (1 - 2 * p)
    return jnp.where(k <= 2 * m, p + near, p + sign * (k - m))


def kernel(
    plan, q_hbm, k_hbm, v_hbm, pattern_ref, table_ref, w_hbm, *rest
):
    dims, orders, cuts, events, n, fused = plan
    if fused:
        out_ref, *rest = rest
    else:
        att_hbm, w_out_hbm, *rest = rest
    (q_ref, k_ref, v_ref, w_ref, wbuf, att, acc, sub, outgoing, incoming, mixb,
     load_sem, own_sem, pair_send, pair_recv, w_send, w_recv, s_send, s_recv, a_send, a_recv) = rest
    me = lax.axis_index("seq")
    core = lax.axis_index("head")
    other = 1 - core
    tokens, width = q_ref.shape
    heads = width // HD
    cols = wbuf.shape[-1]
    bits = n.bit_length() - 1
    groups = a_send.shape[0]
    per = heads // groups
    place = [me // stride % length for length, stride in dims]

    loads = [
        pltpu.make_async_copy(src, dst, load_sem.at[i])
        for i, (src, dst) in enumerate(((w_hbm, w_ref), (k_hbm, k_ref), (v_hbm, v_ref), (q_hbm, q_ref)))
    ]
    for load in loads:
        load.start()

    barrier = pltpu.get_barrier_semaphore()
    total = 1
    pl.semaphore_signal(barrier, inc=1, device_id=(me, other), device_id_type=MESH)
    for bit in range(bits):
        pl.semaphore_signal(barrier, inc=1, device_id=(me ^ (1 << bit), core), device_id_type=MESH)
        total += 1
    for (length, stride), p in zip(dims, place):
        if length == 2:
            continue
        for step in (-1, 1):
            there = jnp.logical_and(p + step >= 0, p + step < length)

            @pl.when(there)
            def _():
                pl.semaphore_signal(barrier, inc=1, device_id=(me + step * stride, core), device_id_type=MESH)

            total = total + there.astype(jnp.int32)

    for l in range(bits + 1):
        if l == 0:
            ids = lax.broadcasted_iota(jnp.int32, (table_ref.shape[0], tokens), 0)
            one_hot = (ids == pattern_ref[...]).astype(jnp.float32)
            mix = lax.dot_general(
                one_hot, table_ref[...], (((0,), (0,)), ((), ())),
                precision=lax.Precision.HIGHEST, preferred_element_type=jnp.float32,
            )
        factor = 1.0 / math.sqrt(tokens * (1 if l == 0 else 2 ** (l - 1)))
        mixb[l] = jnp.broadcast_to(mix[:, l : l + 1] * factor, (tokens, HD))

    def head_cols(h):
        return slice(h * HD, (h + 1) * HD)

    loads[1].wait()
    loads[2].wait()

    def make_states(h):
        state = lax.dot_general(
            k_ref[:, head_cols(h)], v_ref[:, head_cols(h)], (((0,), (0,)), ((), ())),
            preferred_element_type=jnp.float32,
        )
        sub[h] = state
        outgoing[0, h] = state.astype(jnp.bfloat16)

    for h in range(heads):
        make_states(h)
    loads[0].wait()
    pl.semaphore_wait(barrier, total)

    def pair_copy():
        return pltpu.make_async_remote_copy(
            src_ref=w_ref.at[0, :, pl.ds(pl.multiple_of(other * cols, 128), cols)],
            dst_ref=wbuf.at[core, me], send_sem=pair_send, recv_sem=pair_recv,
            device_id=(me, other), device_id_type=MESH,
        )

    def pair_landed():
        return pltpu.make_async_remote_copy(
            src_ref=w_ref.at[0, :, pl.ds(pl.multiple_of(other * cols, 128), cols)],
            dst_ref=wbuf.at[other, me], send_sem=pair_send, recv_sem=pair_recv,
            device_id=(me, other), device_id_type=MESH,
        )

    pair_copy().start()
    own = pltpu.make_async_copy(
        w_ref.at[0, :, pl.ds(pl.multiple_of(core * cols, 128), cols)], wbuf.at[core, me], own_sem
    )
    own.start()

    def state_copy(level, group):
        piece = pl.ds(group * per, per)
        return pltpu.make_async_remote_copy(
            src_ref=outgoing.at[level, piece], dst_ref=incoming.at[level, piece],
            send_sem=s_send.at[level, group], recv_sem=s_recv.at[level, group],
            device_id=(me ^ (1 << level), core), device_id_type=MESH,
        )

    def sum_needed(level):
        return me // 2 ** (level + 1) != n // 2 ** (level + 1) - 1

    def active(level):
        return me // 2**level % 2 == 1

    def sends(level):
        return jnp.logical_or(jnp.logical_not(active(level)), sum_needed(level))

    def receives(level):
        return jnp.logical_or(active(level), sum_needed(level))

    for group in range(groups):
        @pl.when(sends(0))
        def _():
            state_copy(0, group).start()

    def weight_copy(part, source, slot, target):
        lo, size = cuts[part]
        piece = wbuf.at[:, source, :, pl.ds(lo, size)]
        return pltpu.make_async_remote_copy(
            src_ref=piece, dst_ref=piece,
            send_sem=w_send.at[part, source if fused else 0, slot], recv_sem=w_recv.at[part, source],
            device_id=(target, core), device_id_type=MESH,
        )

    def forward(part, source, at, arrived, action):
        order = orders[part]
        for rank in range(max(arrived, 0), len(order)):
            d = order[rank]
            length, stride = dims[d]
            for slot, step in ((2 * rank, 1), (2 * rank + 1, -1)):
                if rank == arrived and length == 2:
                    continue
                ok = jnp.logical_and(place[d] + step >= 0, place[d] + step < length)
                if rank == arrived:
                    ok = jnp.logical_and(ok, (place[d] - at[d]) * step > 0)

                @pl.when(ok)
                def _():
                    copy = weight_copy(part, source, slot, me + step * stride)
                    if action == "start":
                        copy.start()
                    else:
                        copy.wait_send()

    def source_of(part, ks):
        at = {d: nearest(k, place[d], dims[d][0]) for d, k in zip(orders[part], ks)}
        return at, sum(at[d] * dims[d][1] for d in at)

    def arrived_by(ks):
        return max((r for r, k in enumerate(ks) if k), default=-1)

    def weight_event(part, ks, arrived):
        at, source = source_of(part, ks)
        weight_copy(part, source, 0, me).wait_recv()
        forward(part, source, at, arrived, "start")
        if not fused:
            forward(part, source, at, arrived, "wait")

    def read_state(level, h):
        acc[:, head_cols(h)] += mixb[level + 1] * jnp.dot(
            q_ref[:, head_cols(h)], incoming[level, h], preferred_element_type=jnp.float32
        )

    def within_event(h):
        columns = head_cols(h)
        scores = lax.dot_general(
            q_ref[:, columns], k_ref[:, columns], (((1,), (1,)), ((), ())),
            preferred_element_type=jnp.float32,
        )
        row = lax.broadcasted_iota(jnp.int32, (tokens, tokens), 0)
        col = lax.broadcasted_iota(jnp.int32, (tokens, tokens), 1)
        inner = jnp.where(col <= row, scores, 0.0).astype(jnp.bfloat16)
        acc[:, columns] = mixb[0] * jnp.dot(inner, v_ref[:, columns], preferred_element_type=jnp.float32)

    def att_copy(group, mine):
        columns = pl.ds(group * per * HD, per * HD)
        which = core if mine else other
        return pltpu.make_async_remote_copy(
            src_ref=att.at[core, :, columns], dst_ref=att.at[which, :, columns],
            send_sem=a_send.at[group], recv_sem=a_recv.at[group],
            device_id=(me, other), device_id_type=MESH,
        )

    def state_event(level, group):
        @pl.when(receives(level))
        def _():
            state_copy(level, group).wait_recv()

        span = range(group * per, (group + 1) * per)
        if level + 1 < bits:
            @pl.when(sum_needed(level))
            def _():
                for h in span:
                    summed = sub[h] + incoming[level, h].astype(jnp.float32)
                    sub[h] = summed
                    outgoing[level + 1, h] = summed.astype(jnp.bfloat16)

            @pl.when(sends(level + 1))
            def _():
                state_copy(level + 1, group).start()

        @pl.when(active(level))
        def _():
            for h in span:
                read_state(level, h)

        if level + 1 == bits:
            columns = slice(group * per * HD, (group + 1) * per * HD)
            att[core, :, columns] = acc[:, columns].astype(jnp.bfloat16)
            att_copy(group, True).start()

    own.wait()
    pair_landed().wait_recv()
    for part in range(len(orders)):
        at, source = source_of(part, (0,) * len(dims))
        forward(part, source, at, -1, "start")
        if not fused:
            forward(part, source, at, -1, "wait")
    loads[3].wait()

    def project(part):
        lo, size = cuts[part]
        columns = slice(lo, lo + size)
        flat = [wbuf[g, :, :, columns].reshape(-1, size) for g in range(2)]
        out_ref[:, columns] = jnp.dot(att[0], flat[0], preferred_element_type=jnp.float32) + jnp.dot(
            att[1], flat[1], preferred_element_type=jnp.float32
        )

    for event in events:
        if event[0] == "within":
            within_event(event[1])
        elif event[0] == "state":
            state_event(event[1], event[2])
        elif event[0] == "weight":
            weight_event(*event[1:])
        elif event[0] == "loop":
            lengths = [[dims[d][0] for d in order] for order in orders]

            def each(e, carry):
                for part, order in enumerate(orders):
                    for arrived in range(len(order)):
                        below = math.prod(lengths[part][:arrived])
                        ks = []
                        rest_e = e
                        for length in lengths[part]:
                            ks.append(rest_e % length)
                            rest_e = rest_e // length

                        @pl.when(jnp.logical_and(e >= below, e < below * lengths[part][arrived]))
                        def _():
                            weight_event(part, ks, arrived)

                return carry

            lax.fori_loop(1, n, each, 0)
        elif event[0] == "att":
            for group in range(groups):
                att_copy(group, False).wait_recv()
        elif event[0] == "project" and fused:
            project(event[1])

    def finish(part, e):
        ks = []
        for d in orders[part]:
            ks.append(e % dims[d][0])
            e = e // dims[d][0]
        return ks

    pair_copy().wait_send()
    for group in range(groups):
        att_copy(group, True).wait_send()
        for level in range(bits):
            @pl.when(sends(level))
            def _():
                state_copy(level, group).wait_send()
    if fused:
        for part in range(len(orders)):
            for e in range(n):
                ks = finish(part, e)
                at, source = source_of(part, ks)
                forward(part, source, at, arrived_by(ks), "wait")
    if not fused:
        stores = [pltpu.make_async_copy(att, att_hbm, load_sem.at[0]), pltpu.make_async_copy(wbuf, w_out_hbm, load_sem.at[1])]
        for store in stores:
            store.start()
        for store in stores:
            store.wait()


def schedule(dims, orders, cuts, n, heads, groups, unrolled):
    bits = n.bit_length() - 1
    whole = sum(size for _, size in cuts)
    timed = []
    for h in range(heads):
        timed.append((0.35 * h / heads, ("within", h)))
    for level in range(bits):
        for group in range(groups):
            timed.append((0.45 + 0.75 * level + 0.25 * group, ("state", level, group)))
    if not unrolled:
        tail = [("loop",), ("att",)]
    else:
        last = {}
        for part, order in enumerate(orders):
            lengths = [dims[d][0] for d in order]
            count = [0] * len(order)
            for rev in itertools.product(*[range(length) for length in lengths[::-1]]):
                ks = rev[::-1]
                arrived = max((r for r, k in enumerate(ks) if k), default=-1)
                if arrived < 0:
                    continue
                count[arrived] += 1
                when = count[arrived] * cuts[part][1] / whole * 1.8 + 0.3 * sum(1 for k in ks if k)
                if arrived == len(order) - 1 and lengths[-1] == 2:
                    when += 100
                timed.append((when, ("weight", part, ks, arrived)))
        tail = [("att",)]
    timed.sort(key=lambda t: t[0])
    return [e for _, e in timed] + tail + [("project", p) for p in range(len(orders))]


def on_device(dims, queries, keys, values, level_pattern, level_weight, out_weight):
    n = lax.axis_size("seq")
    tokens, width = queries.shape
    heads = width // HD
    bits = n.bit_length() - 1
    _, rows, full = out_weight.shape
    cols = full // 2
    fused = rows % 16 == 0
    groups = min(4, heads)
    tiles = cols // 128
    if len(dims) == 3:
        long = max(range(3), key=lambda i: dims[i][0])
        a, b = [i for i in range(3) if i != long]
        orders = [(long, a, b), (long, b, a), (a, b, long)]
        share = max(1, tiles * 3 // 8)
        sizes = [share, share, tiles - 2 * share]
    else:
        orders, sizes = [tuple(range(len(dims)))], [tiles]
    cuts, lo = [], 0
    for size in sizes:
        cuts.append((lo * 128, size * 128))
        lo += size
    events = schedule(dims, orders, cuts, n, heads, groups, fused)
    plan = (dims, orders, cuts, events, n, fused)
    bf16, f32 = jnp.bfloat16, jnp.float32
    any_spec = pl.BlockSpec(memory_space=pl.ANY)
    vmem_spec = pl.BlockSpec(memory_space=pltpu.VMEM)
    if fused:
        out_shape = jax.ShapeDtypeStruct((tokens, cols), f32)
        out_specs = vmem_spec
    else:
        out_shape = [
            jax.ShapeDtypeStruct((2, tokens, width), bf16),
            jax.ShapeDtypeStruct((2, n, rows, cols), bf16),
        ]
        out_specs = [any_spec, any_spec]
    dma = pltpu.SemaphoreType.DMA
    result = pl.pallas_call(
        functools.partial(kernel, plan),
        out_shape=out_shape,
        in_specs=[any_spec] * 3 + [vmem_spec] * 2 + [any_spec],
        out_specs=out_specs,
        scratch_shapes=[
            pltpu.VMEM((tokens, width), bf16),
            pltpu.VMEM((tokens, width), bf16),
            pltpu.VMEM((tokens, width), bf16),
            pltpu.VMEM((1, rows, full), bf16),
            pltpu.VMEM((2, n, rows, cols), bf16),
            pltpu.VMEM((2, tokens, width), bf16),
            pltpu.VMEM((tokens, width), f32),
            pltpu.VMEM((heads, HD, HD), f32),
            pltpu.VMEM((bits, heads, HD, HD), bf16),
            pltpu.VMEM((bits, heads, HD, HD), bf16),
            pltpu.VMEM((bits + 1, tokens, HD), f32),
            dma((4,)),
            dma,
            dma,
            dma,
            dma((len(orders), n if fused else 1, 2 * len(dims))),
            dma((len(orders), n)),
            dma((bits, groups)),
            dma((bits, groups)),
            dma((groups,)),
            dma((groups,)),
        ],
        compiler_params=pltpu.CompilerParams(
            collective_id=0, has_side_effects=True, vmem_limit_bytes=60 * 2**20
        ),
    )(queries, keys, values, level_pattern.reshape(1, tokens), level_weight, out_weight)
    if fused:
        return result
    att, gathered = result
    return jnp.einsum(
        "gtk,gkd->td", att, gathered.reshape(2, n * rows, cols), preferred_element_type=f32
    )


def solution(mesh):
    placed = (
        P("seq", "head"),
        P("seq", "head"),
        P("seq", "head"),
        P("seq"),
        P(),
        P("head", "seq", None),
    )
    return jax.shard_map(
        functools.partial(on_device, line_dims(mesh)),
        mesh=mesh, in_specs=placed, out_specs=P("seq", "head"), check_vma=False,
    )
```

profile of v0, /device:TPU:28, one launch (start us, length us, event | category | flops | bytes accessed | tf_op | source)
XLA Modules:
  0.0 62.1 jit_solution(15954531961535745736)
XLA Ops:
  0.0 1.2 %reshape.3.pattern_ref = s32[1,384]{1,0:T(1,128)} reshape(s32[384]{0:T(512)} %param.9) | data formatting | bytes 3072 | tf_op jit(solution)/shard_map/reshape | solution.py:440
  1.2 58.2 %shard_map.64 = f32[384,1024]{1,0:T(8,128)} custom-call(bf16[384,1024]{1,0:T(8,128)(2,1)} %q_hbm.1, bf16[384,1024]{1,0:T(8,128)(2,1)} %k_hbm.1, bf16[384,1024]{1,0:T(8,128)(2,1)} %v_hbm.1, s32[1,384]{1,0:T(1,128)} %reshape.3.pattern_ref, f32[16,9]{1,0:T(8,128)} %table_ref.1, bf16[1,64,2048]{2,1,0:T(8,128)(2,1)} %w_hbm.1), custom_call_target="tpu_custom_call" | custom-call | tf_op jit(solution)/shard_map/pallas_call | solution.py:409
  59.4 2.7 %copy.8 = f32[384,1024]{1,0:T(8,128)} copy(f32[384,1024]{1,0:T(8,128)} %shard_map.64) | data formatting | bytes 3145728
where the time goes:
time: 62.4 us; the launch traced here: 62.1 us
  Pallas kernels  58.2 us (93%)
  local copies, waits for them, and re-layouts  3.97 us (6%)
    pallas_call x1, Pallas kernels, on_device(): pl.pallas_call(functools.partial(kernel, plan), out_shape=out_shape, in_s...  58.2 us
    unnamed x1, local copies, waits for them, and re-layouts  2.73 us

commit v1 on v0

--- a/solution.py
+++ b/solution.py
@@ -92,7 +92,7 @@
     for l in range(bits + 1):
         if l == 0:
             ids = lax.broadcasted_iota(jnp.int32, (table_ref.shape[0], tokens), 0)
-            one_hot = (ids == pattern_ref[...]).astype(jnp.float32)
+            one_hot = (ids == pattern_ref[...].reshape(1, tokens)).astype(jnp.float32)
             mix = lax.dot_general(
                 one_hot, table_ref[...], (((0,), (0,)), ((), ())),
                 precision=lax.Precision.HIGHEST, preferred_element_type=jnp.float32,
@@ -397,7 +397,7 @@
     any_spec = pl.BlockSpec(memory_space=pl.ANY)
     vmem_spec = pl.BlockSpec(memory_space=pltpu.VMEM)
     if fused:
-        out_shape = jax.ShapeDtypeStruct((tokens, cols), f32)
+        out_shape = pltpu.VMEM((tokens, cols), f32)
         out_specs = vmem_spec
     else:
         out_shape = [
@@ -437,7 +437,7 @@
         compiler_params=pltpu.CompilerParams(
             collective_id=0, has_side_effects=True, vmem_limit_bytes=60 * 2**20
         ),
-    )(queries, keys, values, level_pattern.reshape(1, tokens), level_weight, out_weight)
+    )(queries, keys, values, level_pattern, level_weight, out_weight)
     if fused:
         return result
     att, gathered = result

time: 62.4 us -> 58.4 us (0.936)
  local copies, waits for them, and re-layouts: 3.97 us -> 1.15 us
  Pallas kernels: 58.2 us -> 57 us
    unnamed x1, local copies, waits for them, and re-layouts: 2.73 us -> 1.15 us
    reshape x1 -> x0, local copies, waits for them, and re-layouts: 1.24 us -> none  [on_device(): level_pattern.reshape(1, tokens)]
    pallas_call x1, Pallas kernels: 58.2 us -> 57 us  [on_device(): pl.pallas_call(functools.partial(kernel, plan), out_shape=out_shape, in_s...]
where the time goes in v1:
time: 58.4 us; the launch traced here: 58.2 us
  Pallas kernels  57 us (98%)
  local copies, waits for them, and re-layouts  1.15 us (2%)
    pallas_call x1, Pallas kernels, on_device(): pl.pallas_call(functools.partial(kernel, plan), out_shape=out_shape, in_s...  57 us

profile of v1, /device:TPU:28, one launch (start us, length us, event | category | flops | bytes accessed | tf_op | source)
XLA Modules:
  0.0 58.2 jit_solution(12661212040430192137)
XLA Ops:
  0.0 57.0 %shard_map.64 = f32[384,1024]{1,0:T(8,128)S(1)} custom-call(bf16[384,1024]{1,0:T(8,128)(2,1)} %q_hbm.1, bf16[384,1024]{1,0:T(8,128)(2,1)} %k_hbm.1, bf16[384,1024]{1,0:T(8,128)(2,1)} %v_hbm.1, s32[384]{0:T(512)} %pattern_ref.1, f32[16,9]{1,0:T(8,128)} %table_ref.1, bf16[1,64,2048]{2,1,0:T(8,128)(2,1)} %w_hbm.1), custom_call_target="tpu_custom_call" | custom-call | tf_op jit(solution)/shard_map/pallas_call | solution.py:409
  57.0 1.1 %copy.8 = f32[384,1024]{1,0:T(8,128)} copy(f32[384,1024]{1,0:T(8,128)S(1)} %shard_map.64) | data formatting | bytes 3145728

commit v2 on v1

--- a/solution.py
+++ b/solution.py
@@ -11,6 +11,9 @@
 
 HD = 128
 MESH = pl.DeviceIdType.MESH
+ORDER = (15, 0, 4, 16, 9, 10, 13, 18, 19, 22, 3, 20, 6, 8, 12, 7, 21, 17, 11, 30, 2, 14, 64, 31, 94, 53, 29, 5, 32, 49, 1, 92, 79, 113, 122, 109, 121, 68, 34, 25, 123, 128, 33, 46, 98, 35, 61, 66, 107, 80, 62, 36, 95, 83, 77, 124, 38, 24, 47, 28, 57, 76, 40, 106, 51, 93, 65, 39, 26, 117, 72, 102, 111, 81, 129, 37, 132, 27, 44, 108, 42, 100, 87, 130, 125, 55, 23, 59, 84, 41, 115, 91, 43, 73, 69, 103, 45, 88, 70, 96, 134, 52, 114, 133, 131, 58, 82, 54, 104, 74, 101, 99, 89, 63, 135, 50, 90, 110, 119, 86, 85, 126, 56, 71, 67, 118, 127, 60, 48, 75, 97, 78, 116, 112, 120, 105,)
+LENGTHS = [4, 2, 2]
+LAG = 6
 
 
 def line_dims(mesh):
@@ -369,6 +372,423 @@
     return [e for _, e in timed] + tail + [("project", p) for p in range(len(orders))]
 
 
+def planned_kernel(
+    plan, q_hbm, k_hbm, v_hbm, pattern_ref, table_ref, w_hbm, out_ref,
+    q_ref, k_ref, v_ref, w_ref, wbuf, att, acc, sub, outgoing, incoming, mixb,
+    load_sem, own_sem, pair_send, pair_recv, w_send, w_recv, s_send, s_recv, a_send, a_recv,
+):
+    dims, parts, events, n = plan
+    me = lax.axis_index("seq")
+    core = lax.axis_index("head")
+    other = 1 - core
+    tokens, width = q_ref.shape
+    rows = w_ref.shape[1]
+    heads = width // HD
+    cols = wbuf.shape[-1]
+    bits = n.bit_length() - 1
+    groups = s_recv.shape[1]
+    per = heads // groups
+    place = [me // stride % length for length, stride in dims]
+
+    loads = {
+        name: pltpu.make_async_copy(src, dst, load_sem.at[i])
+        for i, (name, src, dst) in enumerate(
+            (("w", w_hbm, w_ref), ("k", k_hbm, k_ref), ("v", v_hbm, v_ref), ("q", q_hbm, q_ref))
+        )
+    }
+    for load in loads.values():
+        load.start()
+
+    barrier = pltpu.get_barrier_semaphore()
+    total = 1
+    pl.semaphore_signal(barrier, inc=1, device_id=(me, other), device_id_type=MESH)
+    for (length, stride), p in zip(dims, place):
+        for step in (-1, 1):
+            there = jnp.logical_and(p + step >= 0, p + step < length)
+
+            @pl.when(there)
+            def _():
+                for c in range(2):
+                    pl.semaphore_signal(barrier, inc=1, device_id=(me + step * stride, c), device_id_type=MESH)
+
+            total = total + 2 * there.astype(jnp.int32)
+    for bit in range(bits):
+        if all(1 << bit != stride for _, stride in dims):
+            pl.semaphore_signal(barrier, inc=1, device_id=(me ^ (1 << bit), core), device_id_type=MESH)
+            total = total + 1
+
+    waited = set()
+
+    def loaded(*names):
+        for name in names:
+            if name not in waited:
+                waited.add(name)
+                loads[name].wait()
+
+    loaded("w")
+    pl.semaphore_wait(barrier, total)
+
+    def head_cols(h):
+        return slice(h * HD, (h + 1) * HD)
+
+    def pair_copy(which):
+        return pltpu.make_async_remote_copy(
+            src_ref=w_ref.at[0, :, pl.ds(pl.multiple_of(other * cols, 128), cols)],
+            dst_ref=wbuf.at[which, me], send_sem=pair_send, recv_sem=pair_recv,
+            device_id=(me, other), device_id_type=MESH,
+        )
+
+    own = pltpu.make_async_copy(
+        w_ref.at[0, :, pl.ds(pl.multiple_of(core * cols, 128), cols)], wbuf.at[core, me], own_sem
+    )
+
+    def state_copy(level, group):
+        piece = pl.ds(group * per, per)
+        return pltpu.make_async_remote_copy(
+            src_ref=outgoing.at[level, piece], dst_ref=incoming.at[level, piece],
+            send_sem=s_send.at[level], recv_sem=s_recv.at[level, group],
+            device_id=(me ^ (1 << level), core), device_id_type=MESH,
+        )
+
+    def sum_needed(level):
+        return me // 2 ** (level + 1) != n // 2 ** (level + 1) - 1
+
+    def active(level):
+        return me // 2**level % 2 == 1
+
+    def sends(level):
+        return jnp.logical_or(jnp.logical_not(active(level)), sum_needed(level))
+
+    def receives(level):
+        return jnp.logical_or(active(level), sum_needed(level))
+
+    def first_copy(part, slot, target, half):
+        g, lo, size, _ = parts[part]
+        return pltpu.make_async_remote_copy(
+            src_ref=w_ref.at[0, :, pl.ds(half * cols + lo, size)],
+            dst_ref=wbuf.at[g, me, :, pl.ds(lo, size)],
+            send_sem=w_send.at[part, slot], recv_sem=w_recv.at[part, me],
+            device_id=(target, half), device_id_type=MESH,
+        )
+
+    def first(part, ranks):
+        g, _, _, order = parts[part]
+        for rank in ranks:
+            d = order[rank]
+            length, stride = dims[d]
+            for slot, step in ((2 * rank, 1), (2 * rank + 1, -1)):
+                ok = jnp.logical_and(place[d] + step >= 0, place[d] + step < length)
+
+                @pl.when(jnp.logical_and(ok, core == g))
+                def _():
+                    for half in range(2):
+                        first_copy(part, slot, me + step * stride, half).start()
+
+    def weight_copy(part, source, slot, target):
+        g, lo, size, _ = parts[part]
+        piece = wbuf.at[g, source, :, pl.ds(lo, size)]
+        return pltpu.make_async_remote_copy(
+            src_ref=piece, dst_ref=piece,
+            send_sem=w_send.at[part, slot], recv_sem=w_recv.at[part, source],
+            device_id=(target, core), device_id_type=MESH,
+        )
+
+    def forward(part, ks):
+        order = parts[part][3]
+        at = {d: nearest(k, place[d], dims[d][0]) for d, k in zip(order, ks)}
+        source = sum(at[d] * dims[d][1] for d in at)
+        arrived = max(r for r, k in enumerate(ks) if k)
+        weight_copy(part, source, 0, me).wait_recv()
+        for rank in range(arrived, len(order)):
+            d = order[rank]
+            length, stride = dims[d]
+            for slot, step in ((2 * rank, 1), (2 * rank + 1, -1)):
+                if rank == arrived and length == 2:
+                    continue
+                ok = jnp.logical_and(place[d] + step >= 0, place[d] + step < length)
+                if rank == arrived:
+                    ok = jnp.logical_and(ok, (place[d] - at[d]) * step > 0)
+
+                @pl.when(ok)
+                def _():
+                    weight_copy(part, source, slot, me + step * stride).start()
+
+    def sent(part):
+        g, lo, size, order = parts[part]
+        ahead = 1
+        for rank, d in enumerate(order):
+            length = dims[d][0]
+            for slot, up in ((2 * rank, True), (2 * rank + 1, False)):
+                for p in range(length - 1) if up else range(1, length):
+                    count = ahead - 1 + ahead * (p if up else length - 1 - p)
+                    for mine in (0, 2):
+                        if count + mine == 0:
+                            continue
+
+                        @pl.when(jnp.logical_and(place[d] == p, (core == g) == (mine == 2)))
+                        def _():
+                            piece = wbuf.at[g, pl.ds(0, count + mine), :, pl.ds(lo, size)]
+                            pltpu.make_async_remote_copy(
+                                src_ref=piece, dst_ref=piece, send_sem=w_send.at[part, slot], recv_sem=w_recv.at[part, 0],
+                                device_id=(me, other), device_id_type=MESH,
+                            ).wait_send()
+
+            ahead *= length
+
+    def make_mix():
+        ids = lax.broadcasted_iota(jnp.int32, (table_ref.shape[0], tokens), 0)
+        one_hot = (ids == pattern_ref[...].reshape(1, tokens)).astype(jnp.float32)
+        mix = lax.dot_general(
+            one_hot, table_ref[...], (((0,), (0,)), ((), ())),
+            precision=lax.Precision.HIGHEST, preferred_element_type=jnp.float32,
+        )
+        for l in range(bits + 1):
+            factor = 1.0 / math.sqrt(tokens * (1 if l == 0 else 2 ** (l - 1)))
+            mixb[l] = jnp.broadcast_to(mix[:, l : l + 1] * factor, (tokens, HD))
+
+    def state_start(group):
+        loaded("k", "v")
+        for h in range(group * per, (group + 1) * per):
+            state = lax.dot_general(
+                k_ref[:, head_cols(h)], v_ref[:, head_cols(h)], (((0,), (0,)), ((), ())),
+                preferred_element_type=jnp.float32,
+            )
+            sub[h] = state
+            outgoing[0, h] = state.astype(jnp.bfloat16)
+
+        @pl.when(sends(0))
+        def _():
+            state_copy(0, group).start()
+
+    def within_event(h):
+        columns = head_cols(h)
+        scores = lax.dot_general(
+            q_ref[:, columns], k_ref[:, columns], (((1,), (1,)), ((), ())),
+            preferred_element_type=jnp.float32,
+        )
+        row = lax.broadcasted_iota(jnp.int32, (tokens, tokens), 0)
+        col = lax.broadcasted_iota(jnp.int32, (tokens, tokens), 1)
+        inner = jnp.where(col <= row, scores, 0.0).astype(jnp.bfloat16)
+        acc[:, columns] = mixb[0] * jnp.dot(inner, v_ref[:, columns], preferred_element_type=jnp.float32)
+
+    def att_copy(group):
+        columns = pl.ds(group * per * HD, per * HD)
+        return pltpu.make_async_remote_copy(
+            src_ref=att.at[core, :, columns], dst_ref=att.at[core, :, columns],
+            send_sem=a_send, recv_sem=a_recv,
+            device_id=(me, other), device_id_type=MESH,
+        )
+
+    def att_whole(which):
+        return pltpu.make_async_remote_copy(
+            src_ref=att.at[which], dst_ref=att.at[which], send_sem=a_send, recv_sem=a_recv,
+            device_id=(me, other), device_id_type=MESH,
+        )
+
+    def state_event(level, group):
+        @pl.when(receives(level))
+        def _():
+            state_copy(level, group).wait_recv()
+
+        span = range(group * per, (group + 1) * per)
+        if level + 1 < bits:
+            @pl.when(sum_needed(level))
+            def _():
+                for h in span:
+                    summed = sub[h] + incoming[level, h].astype(jnp.float32)
+                    sub[h] = summed
+                    outgoing[level + 1, h] = summed.astype(jnp.bfloat16)
+
+            @pl.when(sends(level + 1))
+            def _():
+                state_copy(level + 1, group).start()
+
+    def read_event(level, group):
+        @pl.when(active(level))
+        def _():
+            for h in range(group * per, (group + 1) * per):
+                acc[:, head_cols(h)] += mixb[level + 1] * jnp.dot(
+                    q_ref[:, head_cols(h)], incoming[level, h], preferred_element_type=jnp.float32
+                )
+
+        if level + 1 == bits:
+            columns = slice(group * per * HD, (group + 1) * per * HD)
+            att[core, :, columns] = acc[:, columns].astype(jnp.bfloat16)
+            att_copy(group).start()
+
+    def project(part, k):
+        g, lo, size, _ = parts[part]
+        length, stride = dims[0]
+        slab = nearest(k, place[0], length) * stride
+        depth = stride * rows
+        piece = wbuf[g, pl.ds(slab, stride), :, lo : lo + size].reshape(depth, size)
+        taken = att[g, :, pl.ds(pl.multiple_of(slab * rows, math.gcd(depth, 1024)), depth)]
+        out_ref[:, lo : lo + size] += jnp.dot(taken, piece, preferred_element_type=jnp.float32)
+
+    for event in events:
+        kind, args = event[0], event[1:]
+        if kind == "first":
+            first(*args)
+        elif kind == "pair":
+            pair_copy(core).start()
+            own.start()
+        elif kind == "paired":
+            own.wait()
+            pair_copy(other).wait_recv()
+        elif kind == "start":
+            state_start(*args)
+        elif kind == "mix":
+            make_mix()
+            out_ref[...] = jnp.zeros_like(out_ref)
+        elif kind == "within":
+            loaded("k", "v", "q")
+            within_event(*args)
+        elif kind == "state":
+            state_event(*args)
+        elif kind == "read":
+            read_event(*args)
+        elif kind == "weight":
+            forward(*args)
+        elif kind == "att":
+            att_whole(other).wait_recv()
+        elif kind == "project":
+            project(*args)
+
+    pair_copy(core).wait_send()
+    att_whole(core).wait_send()
+    for level in range(bits):
+        @pl.when(sends(level))
+        def _():
+            pltpu.make_async_remote_copy(
+                src_ref=outgoing.at[level], dst_ref=incoming.at[level],
+                send_sem=s_send.at[level], recv_sem=s_recv.at[level, 0],
+                device_id=(me ^ (1 << level), core), device_id_type=MESH,
+            ).wait_send()
+    for part in range(len(parts)):
+        sent(part)
+
+
+def make_parts(dims, tiles):
+    long = max(range(3), key=lambda i: dims[i][0])
+    a, b = [i for i in range(3) if i != long]
+    direct = max(1, tiles // 8)
+    most = (tiles - direct + 1) // 2
+    parts = []
+    for g, sizes in enumerate(((most, tiles - direct - most, direct), (tiles - direct - most, most, direct))):
+        last = (b, a, long) if g == 0 else (a, b, long)
+        lo = 0
+        for size, order in zip(sizes, ((long, b, a), (long, a, b), last)):
+            parts.append((g, lo * 128, size * 128, order))
+            lo += size
+    return parts
+
+
+def make_events(dims, parts, n, heads, groups):
+    bits = n.bit_length() - 1
+    timed = []
+    for part, (_, _, _, order) in enumerate(parts):
+        for rank, d in enumerate(order):
+            timed.append(((0, rank, part), ("first", part, (rank,))))
+    for group in range(groups):
+        timed.append(((1, group), ("start", group)))
+    for h in range(heads):
+        timed.append(((3 + h, 9), ("within", h)))
+    for level in range(bits):
+        for group in range(groups):
+            timed.append(((3 + 3 * level + group, 0), ("state", level, group)))
+    for part, (_, _, _, order) in enumerate(parts):
+        for ks in itertools.product(*[range(dims[d][0]) for d in order]):
+            if any(ks):
+                timed.append(((3 * sum(1 for k in ks if k) + sum(ks), part), ("weight", part, ks)))
+    if ORDER and len(ORDER) == len(timed) and [d[0] for d in dims] == LENGTHS:
+        chosen = [timed[i][1] for i in ORDER]
+    else:
+        chosen = [event for _, event in sorted(timed, key=lambda t: t[0])]
+    events, inside = [], []
+    for event in chosen:
+        if event[0] == "within" and event[1] in inside:
+            continue
+        due = [event[1]] if event[0] == "within" else []
+        if event[0] == "state":
+            events.append(event)
+            per = heads // groups
+            due = [h for h in range(event[2] * per, (event[2] + 1) * per) if h not in inside]
+        if due and not inside:
+            events.append(("mix",))
+        events += [("within", h) for h in due]
+        inside += due
+        if event[0] == "state":
+            events.append(("read",) + event[1:])
+        elif event[0] != "within":
+            events.append(event)
+    at = 1 + max(i for i, e in enumerate(events) if e[0] == "start")
+    events.insert(at, ("pair",))
+    reads = max(i for i, e in enumerate(events) if e[0] == "read")
+    at = min(len(events), reads + 1 + LAG)
+    events[at:at] = [("paired",), ("att",)]
+    ready = {}
+    for i, e in enumerate(events):
+        if e[0] == "weight":
+            key = (e[1], e[2][parts[e[1]][3].index(0)])
+            ready[key] = max(ready.get(key, at + 1), i)
+    placed, queue = [], []
+    for i, e in enumerate(events):
+        placed.append(e)
+        queue += sorted((key for key, j in ready.items() if j == i), key=lambda key: key[::-1])
+        if queue and i + 1 < len(events):
+            placed.append(("project",) + queue.pop(0))
+    placed += [("project",) + key for key in queue]
+    return placed
+
+
+def planned(dims, queries, keys, values, level_pattern, level_weight, out_weight):
+    n = lax.axis_size("seq")
+    tokens, width = queries.shape
+    heads = width // HD
+    bits = n.bit_length() - 1
+    _, rows, full = out_weight.shape
+    cols = full // 2
+    groups = min(4, heads)
+    parts = make_parts(dims, cols // 128)
+    events = make_events(dims, parts, n, heads, groups)
+    bf16, f32 = jnp.bfloat16, jnp.float32
+    any_spec = pl.BlockSpec(memory_space=pl.ANY)
+    vmem_spec = pl.BlockSpec(memory_space=pltpu.VMEM)
+    dma = pltpu.SemaphoreType.DMA
+    return pl.pallas_call(
+        functools.partial(planned_kernel, (dims, parts, events, n)),
+        out_shape=pltpu.VMEM((tokens, cols), f32),
+        in_specs=[any_spec] * 3 + [vmem_spec] * 2 + [any_spec],
+        out_specs=vmem_spec,
+        scratch_shapes=[
+            pltpu.VMEM((tokens, width), bf16),
+            pltpu.VMEM((tokens, width), bf16),
+            pltpu.VMEM((tokens, width), bf16),
+            pltpu.VMEM((1, rows, full), bf16),
+            pltpu.VMEM((2, n, rows, cols), bf16),
+            pltpu.VMEM((2, tokens, width), bf16),
+            pltpu.VMEM((tokens, width), f32),
+            pltpu.VMEM((heads, HD, HD), f32),
+            pltpu.VMEM((bits, heads, HD, HD), bf16),
+            pltpu.VMEM((bits, heads, HD, HD), bf16),
+            pltpu.VMEM((bits + 1, tokens, HD), f32),
+            dma((4,)),
+            dma,
+            dma,
+            dma,
+            dma((len(parts), 2 * len(dims))),
+            dma((len(parts), n)),
+            dma((bits,)),
+            dma((bits, groups)),
+            dma,
+            dma,
+        ],
+        compiler_params=pltpu.CompilerParams(
+            collective_id=0, has_side_effects=True, vmem_limit_bytes=60 * 2**20
+        ),
+    )(queries, keys, values, level_pattern, level_weight, out_weight)
+
+
 def on_device(dims, queries, keys, values, level_pattern, level_weight, out_weight):
     n = lax.axis_size("seq")
     tokens, width = queries.shape
@@ -377,6 +797,8 @@
     _, rows, full = out_weight.shape
     cols = full // 2
     fused = rows % 16 == 0
+    if fused and len(dims) == 3 and cols % 1024 == 0:
+        return planned(dims, queries, keys, values, level_pattern, level_weight, out_weight)
     groups = min(4, heads)
     tiles = cols // 128
     if len(dims) == 3:

time: 58.4 us -> 54 us (0.925)
  the two profiles are of different devices: /device:TPU:28 before, /device:TPU:0 now
where the time goes in v2:
time: 54 us; the launch traced here: 53.8 us
  Pallas kernels  52.6 us (97%)
  local copies, waits for them, and re-layouts  1.15 us (2%)
    pallas_call x1, Pallas kernels, planned(): pl.pallas_call(functools.partial(planned_kernel, (dims, parts, events, n)...  52.6 us
    unnamed x1, local copies, waits for them, and re-layouts  1.15 us

profile of v2, /device:TPU:0, one launch (start us, length us, event | category | flops | bytes accessed | tf_op | source)
XLA Modules:
  0.0 53.8 jit_solution(9769100229938990485)
XLA Ops:
  0.0 52.6 %shard_map.64 = f32[384,1024]{1,0:T(8,128)S(1)} custom-call(bf16[384,1024]{1,0:T(8,128)(2,1)} %q_hbm.1, bf16[384,1024]{1,0:T(8,128)(2,1)} %k_hbm.1, bf16[384,1024]{1,0:T(8,128)(2,1)} %v_hbm.1, s32[384]{0:T(512)} %pattern_ref.1, f32[16,9]{1,0:T(8,128)} %table_ref.1, bf16[1,64,2048]{2,1,0:T(8,128)(2,1)} %w_hbm.1), custom_call_target="tpu_custom_call" | custom-call | tf_op jit(solution)/shard_map/pallas_call | solution.py:758
  52.7 1.1 %copy.8 = f32[384,1024]{1,0:T(8,128)} copy(f32[384,1024]{1,0:T(8,128)S(1)} %shard_map.64) | data formatting | bytes 3145728

commit v3 on v2

--- a/solution.py
+++ b/solution.py
@@ -412,7 +412,7 @@
                     pl.semaphore_signal(barrier, inc=1, device_id=(me + step * stride, c), device_id_type=MESH)
 
             total = total + 2 * there.astype(jnp.int32)
-    for bit in range(bits):
+    for bit in range(bits - 1):
         if all(1 << bit != stride for _, stride in dims):
             pl.semaphore_signal(barrier, inc=1, device_id=(me ^ (1 << bit), core), device_id_type=MESH)
             total = total + 1
@@ -442,25 +442,37 @@
         w_ref.at[0, :, pl.ds(pl.multiple_of(core * cols, 128), cols)], wbuf.at[core, me], own_sem
     )
 
-    def state_copy(level, group):
+    top = bits - 1
+    reach, climb = dims[0]
+
+    def state_copy(level, group, relay=False):
         piece = pl.ds(group * per, per)
-        return pltpu.make_async_remote_copy(
-            src_ref=outgoing.at[level, piece], dst_ref=incoming.at[level, piece],
+        target = me + climb if level == top else me ^ (1 << level)
+        return pltpu.make_async_remote_copy(
+            src_ref=(incoming if relay else outgoing).at[level, piece], dst_ref=incoming.at[level, piece],
             send_sem=s_send.at[level], recv_sem=s_recv.at[level, group],
-            device_id=(me ^ (1 << level), core), device_id_type=MESH,
-        )
-
-    def sum_needed(level):
-        return me // 2 ** (level + 1) != n // 2 ** (level + 1) - 1
-
-    def active(level):
-        return me // 2**level % 2 == 1
+            device_id=(target, core), device_id_type=MESH,
+        )
+
+    def sum_needed(level, who=me):
+        if level == top - 1:
+            return who // climb == reach // 2 - 1
+        return who // 2 ** (level + 1) != n // 2 ** (level + 1) - 1
+
+    def active(level, who=me):
+        return who // 2**level % 2 == 1
+
+    def receives(level, who=me):
+        if level == top:
+            return active(level, who)
+        return jnp.logical_or(active(level, who), sum_needed(level, who))
 
     def sends(level):
-        return jnp.logical_or(jnp.logical_not(active(level)), sum_needed(level))
-
-    def receives(level):
-        return jnp.logical_or(active(level), sum_needed(level))
+        if level == top:
+            return place[0] == reach // 2 - 1
+        return receives(level, me ^ (1 << level))
+
+    relays = jnp.logical_and(active(top), place[0] < reach - 1)
 
     def first_copy(part, slot, target, half):
         g, lo, size, _ = parts[part]
@@ -602,6 +614,10 @@
             @pl.when(sends(level + 1))
             def _():
                 state_copy(level + 1, group).start()
+        else:
+            @pl.when(relays)
+            def _():
+                state_copy(level, group, True).start()
 
     def read_event(level, group):
         @pl.when(active(level))
@@ -657,7 +673,7 @@
     pair_copy(core).wait_send()
     att_whole(core).wait_send()
     for level in range(bits):
-        @pl.when(sends(level))
+        @pl.when(jnp.logical_or(sends(level), relays) if level == top else sends(level))
         def _():
             pltpu.make_async_remote_copy(
                 src_ref=outgoing.at[level], dst_ref=incoming.at[level],

time: 54 us -> 53.3 us (0.987)
  Pallas kernels: 52.6 us -> 52 us
    pallas_call x1, Pallas kernels: 52.6 us -> 52 us  [planned(): pl.pallas_call(functools.partial(planned_kernel, (dims, parts, events, n)...]
where the time goes in v3:
time: 53.3 us; the launch traced here: 53.1 us
  Pallas kernels  52 us (98%)
  local copies, waits for them, and re-layouts  1.15 us (2%)
    pallas_call x1, Pallas kernels, planned(): pl.pallas_call(functools.partial(planned_kernel, (dims, parts, events, n)...  52 us
    unnamed x1, local copies, waits for them, and re-layouts  1.15 us

profile of v3, /device:TPU:0, one launch (start us, length us, event | category | flops | bytes accessed | tf_op | source)
XLA Modules:
  0.0 53.1 jit_solution(14948693339147004686)
XLA Ops:
  0.0 52.0 %shard_map.64 = f32[384,1024]{1,0:T(8,128)S(1)} custom-call(bf16[384,1024]{1,0:T(8,128)(2,1)} %q_hbm.1, bf16[384,1024]{1,0:T(8,128)(2,1)} %k_hbm.1, bf16[384,1024]{1,0:T(8,128)(2,1)} %v_hbm.1, s32[384]{0:T(512)} %pattern_ref.1, f32[16,9]{1,0:T(8,128)} %table_ref.1, bf16[1,64,2048]{2,1,0:T(8,128)(2,1)} %w_hbm.1), custom_call_target="tpu_custom_call" | custom-call | tf_op jit(solution)/shard_map/pallas_call | solution.py:774
  52.0 1.1 %copy.8 = f32[384,1024]{1,0:T(8,128)} copy(f32[384,1024]{1,0:T(8,128)S(1)} %shard_map.64) | data formatting | bytes 3145728

commit v4 on v3

--- a/solution.py
+++ b/solution.py
@@ -11,7 +11,7 @@
 
 HD = 128
 MESH = pl.DeviceIdType.MESH
-ORDER = (15, 0, 4, 16, 9, 10, 13, 18, 19, 22, 3, 20, 6, 8, 12, 7, 21, 17, 11, 30, 2, 14, 64, 31, 94, 53, 29, 5, 32, 49, 1, 92, 79, 113, 122, 109, 121, 68, 34, 25, 123, 128, 33, 46, 98, 35, 61, 66, 107, 80, 62, 36, 95, 83, 77, 124, 38, 24, 47, 28, 57, 76, 40, 106, 51, 93, 65, 39, 26, 117, 72, 102, 111, 81, 129, 37, 132, 27, 44, 108, 42, 100, 87, 130, 125, 55, 23, 59, 84, 41, 115, 91, 43, 73, 69, 103, 45, 88, 70, 96, 134, 52, 114, 133, 131, 58, 82, 54, 104, 74, 101, 99, 89, 63, 135, 50, 90, 110, 119, 86, 85, 126, 56, 71, 67, 118, 127, 60, 48, 75, 97, 78, 116, 112, 120, 105,)
+ORDER = (13, 16, 12, 7, 4, 18, 6, 17, 0, 15, 19, 10, 25, 3, 22, 9, 27, 21, 20, 23, 11, 79, 5, 30, 29, 24, 31, 91, 49, 8, 64, 2, 26, 128, 53, 94, 34, 32, 122, 1, 109, 28, 61, 35, 113, 33, 98, 66, 83, 92, 121, 107, 39, 80, 124, 51, 77, 65, 68, 57, 130, 54, 62, 14, 38, 132, 95, 115, 81, 76, 47, 36, 129, 37, 87, 46, 43, 117, 134, 40, 52, 102, 67, 133, 72, 69, 44, 106, 70, 41, 123, 42, 103, 84, 55, 96, 59, 74, 119, 89, 88, 45, 118, 82, 131, 93, 108, 100, 111, 78, 116, 104, 85, 114, 125, 63, 97, 126, 99, 90, 86, 58, 48, 135, 50, 73, 120, 75, 56, 60, 127, 101, 110, 112, 105, 71,)
 LENGTHS = [4, 2, 2]
 LAG = 6
 

time: 53.3 us -> 51.8 us (0.972)
  Pallas kernels: 52 us -> 50.5 us
    pallas_call x1, Pallas kernels: 52 us -> 50.5 us  [planned(): pl.pallas_call(functools.partial(planned_kernel, (dims, parts, events, n)...]
where the time goes in v4:
time: 51.8 us; the launch traced here: 51.6 us
  Pallas kernels  50.5 us (97%)
  local copies, waits for them, and re-layouts  1.15 us (2%)
    pallas_call x1, Pallas kernels, planned(): pl.pallas_call(functools.partial(planned_kernel, (dims, parts, events, n)...  50.5 us
    unnamed x1, local copies, waits for them, and re-layouts  1.15 us

profile of v4, /device:TPU:0, one launch (start us, length us, event | category | flops | bytes accessed | tf_op | source)
XLA Modules:
  0.0 51.6 jit_solution(15632610034200107518)
XLA Ops:
  0.0 50.5 %shard_map.64 = f32[384,1024]{1,0:T(8,128)S(1)} custom-call(bf16[384,1024]{1,0:T(8,128)(2,1)} %q_hbm.1, bf16[384,1024]{1,0:T(8,128)(2,1)} %k_hbm.1, bf16[384,1024]{1,0:T(8,128)(2,1)} %v_hbm.1, s32[384]{0:T(512)} %pattern_ref.1, f32[16,9]{1,0:T(8,128)} %table_ref.1, bf16[1,64,2048]{2,1,0:T(8,128)(2,1)} %w_hbm.1), custom_call_target="tpu_custom_call" | custom-call | tf_op jit(solution)/shard_map/pallas_call | solution.py:774
  50.5 1.1 %copy.8 = f32[384,1024]{1,0:T(8,128)} copy(f32[384,1024]{1,0:T(8,128)S(1)} %shard_map.64) | data formatting | bytes 3145728

commit v5 on v4

--- a/solution.py
+++ b/solution.py
@@ -11,7 +11,7 @@
 
 HD = 128
 MESH = pl.DeviceIdType.MESH
-ORDER = (13, 16, 12, 7, 4, 18, 6, 17, 0, 15, 19, 10, 25, 3, 22, 9, 27, 21, 20, 23, 11, 79, 5, 30, 29, 24, 31, 91, 49, 8, 64, 2, 26, 128, 53, 94, 34, 32, 122, 1, 109, 28, 61, 35, 113, 33, 98, 66, 83, 92, 121, 107, 39, 80, 124, 51, 77, 65, 68, 57, 130, 54, 62, 14, 38, 132, 95, 115, 81, 76, 47, 36, 129, 37, 87, 46, 43, 117, 134, 40, 52, 102, 67, 133, 72, 69, 44, 106, 70, 41, 123, 42, 103, 84, 55, 96, 59, 74, 119, 89, 88, 45, 118, 82, 131, 93, 108, 100, 111, 78, 116, 104, 85, 114, 125, 63, 97, 126, 99, 90, 86, 58, 48, 135, 50, 73, 120, 75, 56, 60, 127, 101, 110, 112, 105, 71,)
+ORDER = (3, 15, 10, 9, 11, 6, 12, 18, 20, 19, 29, 2, 26, 24, 21, 7, 23, 94, 0, 4, 17, 25, 28, 27, 22, 30, 14, 32, 16, 98, 13, 109, 113, 31, 83, 34, 49, 33, 95, 8, 92, 53, 64, 79, 128, 122, 38, 68, 36, 107, 77, 121, 102, 91, 117, 72, 124, 76, 35, 1, 51, 84, 129, 37, 5, 132, 40, 39, 123, 87, 62, 57, 42, 80, 114, 111, 100, 106, 108, 115, 69, 54, 134, 73, 104, 99, 41, 43, 66, 93, 88, 50, 47, 81, 133, 44, 45, 130, 125, 131, 119, 63, 96, 110, 59, 89, 90, 74, 135, 126, 55, 61, 78, 46, 101, 112, 82, 70, 85, 127, 105, 58, 67, 118, 65, 116, 120, 103, 48, 75, 60, 86, 52, 71, 56, 97,)
 LENGTHS = [4, 2, 2]
 LAG = 6
 

time: 51.8 us -> 50.3 us (0.971)
  Pallas kernels: 50.5 us -> 48.9 us
    pallas_call x1, Pallas kernels: 50.5 us -> 48.9 us  [planned(): pl.pallas_call(functools.partial(planned_kernel, (dims, parts, events, n)...]
where the time goes in v5:
time: 50.3 us; the launch traced here: 50.1 us
  Pallas kernels  48.9 us (97%)
  local copies, waits for them, and re-layouts  1.15 us (2%)
    pallas_call x1, Pallas kernels, planned(): pl.pallas_call(functools.partial(planned_kernel, (dims, parts, events, n)...  48.9 us
    unnamed x1, local copies, waits for them, and re-layouts  1.15 us

profile of v5, /device:TPU:0, one launch (start us, length us, event | category | flops | bytes accessed | tf_op | source)
XLA Modules:
  0.0 50.1 jit_solution(2316762368315080754)
XLA Ops:
  0.0 48.9 %shard_map.64 = f32[384,1024]{1,0:T(8,128)S(1)} custom-call(bf16[384,1024]{1,0:T(8,128)(2,1)} %q_hbm.1, bf16[384,1024]{1,0:T(8,128)(2,1)} %k_hbm.1, bf16[384,1024]{1,0:T(8,128)(2,1)} %v_hbm.1, s32[384]{0:T(512)} %pattern_ref.1, f32[16,9]{1,0:T(8,128)} %table_ref.1, bf16[1,64,2048]{2,1,0:T(8,128)(2,1)} %w_hbm.1), custom_call_target="tpu_custom_call" | custom-call | tf_op jit(solution)/shard_map/pallas_call | solution.py:774
  48.9 1.1 %copy.8 = f32[384,1024]{1,0:T(8,128)} copy(f32[384,1024]{1,0:T(8,128)S(1)} %shard_map.64) | data formatting | bytes 3145728
